TPU v7x, 256 devices: a whole 4x4x8 slice. The times are simulated.
256 devices in a mesh: seq: 16 (over y, z_hi, core), mp: 16 (over z_lo, x).
Axes of the slice: x: 4, y: 4, z: 8 (z_hi: 2, z_lo: 4; z = z_hi * 4 + z_lo), core: 2. Of those that a mesh axis runs over, the one named last changes fastest.
Arguments:
- hidden_in: bfloat16 [2048, 2048], P('seq'), may hold values from -0.59765625 to 0.59765625
- input_gain: float32 [2048], replicated, may hold values from 0.25 to 1.75
- w_query: bfloat16 [2048, 2048], P(None, 'mp'), may hold values from -0.125 to 0.125
- key_value_weight: bfloat16 [2048, 4096], P(None, 'mp'), may hold values from -1 to 1, as said below
- query_gain: float32 [128], replicated, may hold values from 0.25 to 1.75
- key_gain: float32 [128], replicated, may hold values from 0.25 to 1.75
- w_out: bfloat16 [2048, 2048], P('mp'), may hold values from -0.125 to 0.125
- post_gain: float32 [2048], replicated, may hold values from 0.25 to 1.75
- w_gate: bfloat16 [2048, 6144], P(None, 'mp'), may hold values from -0.125 to 0.125
- w_up: bfloat16 [2048, 6144], P(None, 'mp'), may hold values from -0.125 to 0.125
- w_down: bfloat16 [6144, 2048], P('mp'), may hold values from -0.078125 to 0.078125
- prefix_slot_cache: bfloat16 [32, 256, 8, 256], P('seq'), may hold values from -240 to 240, as said below
- block_table: int32 [32], replicated, may hold values from 0 to 31, each once
- request_prefix: int32 [32], replicated, may hold values from 0 to 3
- suffix_lengths: int32 [32], replicated, may hold values from 1 to 256, 2048 in all
Outputs:
- hidden_out: bfloat16 [2048, 2048], P('seq', 'mp')
- suffix_key_values: bfloat16 [2048, 2048], P('seq', 'mp')
Inputs may be any that keep to these rules, and one draw needn't show every extreme that they name: block_table[p * 8 + i] is the slot holding block i of prefix p; every slot appears once. `suffix_lengths`: the lengths add up to 2048 and the longest is exactly 256. `prefix_slot_cache`: per slot, position and key-value head: a key in the first 128 entries, a value in the last 128. `key_value_weight`: columns of key-value head k: 2 equal blocks of 256, starting at k * 2 * 2 * 128.
All inputs are finite; a program needn't handle non-finite values.
Results may differ from a plain program's by a relative error of at most 0.025.
The roundings to bfloat16 on the way count: a program that leaves them out, or rounds other values in their place, can miss the bound.
Values may be sent and summed in bfloat16 or wider, within the bound.
A program may use at most 64 MiB of HBM per device.

v0:
```python
import math
import jax
import jax.numpy as jnp
from jax import lax
from jax.sharding import PartitionSpec as P

QUERY_HEADS = 16
KEY_VALUE_HEADS = 8
HEAD_WIDTH = 128
N_PREFIX = 4
EPSILON = 1e-06
THETA = 1000000.0
NEGATIVE_FLOOR = -1e30


def token_tables(request_prefix, suffix_lengths, positions, prefix_length):
    request_ends = jnp.cumsum(suffix_lengths)
    starts = request_ends - suffix_lengths
    inside = (
        (positions[:, None] >= starts[None, :]) & (positions[:, None] < request_ends[None, :])
    ).astype(jnp.int32)
    request_ids = jnp.arange(suffix_lengths.shape[0], dtype=jnp.int32)
    request_of = jnp.sum(inside * request_ids[None, :], axis=1)
    start_of = jnp.sum(inside * starts[None, :], axis=1)
    prefix_of = jnp.sum(inside * request_prefix[None, :], axis=1)
    rotary_pos = prefix_length + positions - start_of
    return (request_of, prefix_of, rotary_pos)


def row_norm(values, gain):
    return values * lax.rsqrt(jnp.mean(values * values, axis=-1, keepdims=True) + EPSILON) * gain


def head_norm(values, gain):
    return values * lax.rsqrt(jnp.mean(values * values, axis=-1, keepdims=True) + EPSILON) * gain


def rotate(values, rotary_pos):
    half_dim = values.shape[-1] // 2
    freq_ids = jnp.arange(half_dim).astype(jnp.float32)
    inverse = jnp.exp(freq_ids * (-2.0 * math.log(THETA) / values.shape[-1]))
    angles = rotary_pos.astype(jnp.float32)[:, None] * inverse[None, :]
    cosine = jnp.cos(angles)[:, None, :]
    sine_part = jnp.sin(angles)[:, None, :]
    first_half = values[..., :half_dim]
    second_half = values[..., half_dim:]
    return jnp.concatenate(
        [
            first_half * cosine - second_half * sine_part,
            second_half * cosine + first_half * sine_part,
        ],
        axis=-1,
    )


def allowed_keys(query_req, query_pre, query_pos, key_pre, key_req, key_pos):
    same_prefix = key_pre[None, :] == query_pre[:, None]
    same_request = (key_req[None, :] == query_req[:, None]) & (
        key_pos[None, :] <= query_pos[:, None]
    )
    return same_prefix | same_request


def group_partial(query_rows_all, allowed, key_row_block, value_row_block):
    scaling = 1.0 / math.sqrt(query_rows_all.shape[-1])
    scores = (
        jnp.einsum(
            "nkgd,mkd->nkgm", query_rows_all, key_row_block, preferred_element_type=jnp.float32
        )
        * scaling
    )
    allowed_full = allowed[:, None, None, :]
    scores = jnp.where(allowed_full, scores, NEGATIVE_FLOOR)
    highest_score = jnp.max(scores, axis=-1)
    weights = jnp.where(allowed_full, jnp.exp(scores - highest_score[..., None]), 0.0)
    total_weight = jnp.sum(weights, axis=-1)
    rounded = weights.astype(jnp.bfloat16)
    summed = jnp.einsum(
        "nkgm,mkd->nkgd", rounded, value_row_block, preferred_element_type=jnp.float32
    )
    layer_output = (summed / jnp.maximum(total_weight, 1.0)[..., None]).astype(jnp.bfloat16)
    return (highest_score, total_weight, layer_output)


def tile_partials(query_rows, query_req, query_pre, query_pos, bundle, tile_rows):
    key_row_block, value_row_block, key_pre, key_req, key_pos = bundle
    token_count = query_rows.shape[0]
    tile_count = token_count // tile_rows
    shaped = (
        query_rows.reshape((tile_count, tile_rows) + query_rows.shape[1:]),
        query_req.reshape(tile_count, tile_rows),
        query_pre.reshape(tile_count, tile_rows),
        query_pos.reshape(tile_count, tile_rows),
    )

    def one_tile(members):
        tile_queries, tile_req, tile_pre, tile_pos = members
        allowed = allowed_keys(tile_req, tile_pre, tile_pos, key_pre, key_req, key_pos)

        def computed(unused):
            return group_partial(tile_queries, allowed, key_row_block, value_row_block)

        def skipped(unused):
            stats_shape = tile_queries.shape[:-1]
            return (
                jnp.full(stats_shape, NEGATIVE_FLOOR, jnp.float32),
                jnp.zeros(stats_shape, jnp.float32),
                jnp.zeros(tile_queries.shape, jnp.bfloat16),
            )

        return lax.cond(jnp.any(allowed), computed, skipped, 0)

    highest_score, total_weight, layer_output = lax.map(one_tile, shaped)
    stats_shape = (token_count,) + query_rows.shape[1:-1]
    return (
        highest_score.reshape(stats_shape),
        total_weight.reshape(stats_shape),
        layer_output.reshape(query_rows.shape),
    )


def local(
    hidden_in,
    input_gain,
    w_query,
    key_value_weight,
    query_gain,
    key_gain,
    w_out,
    post_gain,
    w_gate,
    w_up,
    w_down,
    prefix_slot_cache,
    block_table,
    request_prefix,
    suffix_lengths,
):
    seq_count = lax.axis_size("seq")
    model_count = lax.axis_size("mp")
    my_seq = lax.axis_index("seq")
    my_model = lax.axis_index("mp")
    rows_here = hidden_in.shape[0]
    local_heads = w_query.shape[1] // HEAD_WIDTH
    group_width = QUERY_HEADS // KEY_VALUE_HEADS
    shared_heads = max(1, local_heads // group_width)
    query_per_head = local_heads // shared_heads
    pair_width = 2 * HEAD_WIDTH
    first_shared = my_model * local_heads // group_width
    blocks_here = prefix_slot_cache.shape[0]
    block_rows = prefix_slot_cache.shape[1]
    cache_extent = blocks_here * block_rows
    slot_total = blocks_here * seq_count
    prefix_length = slot_total // N_PREFIX * block_rows
    all_tokens = rows_here * seq_count
    hidden_f32 = hidden_in.astype(jnp.float32)
    normed = row_norm(hidden_f32, input_gain).astype(jnp.bfloat16)
    own_pos = my_seq * rows_here + jnp.arange(rows_here, dtype=jnp.int32)
    own_req, own_pre, own_rot = token_tables(request_prefix, suffix_lengths, own_pos, prefix_length)
    query_raw = jnp.dot(normed, w_query, preferred_element_type=jnp.float32).reshape(
        rows_here, local_heads, HEAD_WIDTH
    )
    query_rows_all = rotate(head_norm(query_raw, query_gain), own_rot).astype(jnp.bfloat16)
    pair_block = jnp.dot(normed, key_value_weight, preferred_element_type=jnp.float32).astype(
        jnp.bfloat16
    )
    share_ratio = max(1, group_width // local_heads)
    pair_split = pair_block.reshape(rows_here, shared_heads, 2, HEAD_WIDTH)
    key_row_block = rotate(
        head_norm(pair_split[:, :, 0].astype(jnp.float32), key_gain), own_rot
    ).astype(jnp.bfloat16)
    pairs_mine = jnp.stack([key_row_block, pair_split[:, :, 1]], axis=2).reshape(
        rows_here, shared_heads, pair_width
    )
    cache_cols = shared_heads * pair_width // share_ratio
    suffix_key_values = lax.dynamic_slice_in_dim(
        pairs_mine.reshape(rows_here, shared_heads * pair_width),
        my_model % share_ratio * cache_cols,
        cache_cols,
        1,
    )
    slot_ids = jnp.arange(slot_total, dtype=jnp.int32)
    owner_hits = (block_table[:, None] == slot_ids[None, :]).astype(jnp.int32)
    slot_prefix = jnp.sum(owner_hits * (slot_ids // (slot_total // N_PREFIX))[:, None], axis=0)
    cache_mine = lax.dynamic_slice_in_dim(prefix_slot_cache, first_shared, shared_heads, 2).reshape(
        cache_extent, shared_heads, pair_width
    )
    query_all = lax.all_gather(
        query_rows_all.reshape(rows_here, local_heads * HEAD_WIDTH), "seq", axis=0, tiled=True
    )
    query_all = query_all.reshape(all_tokens, shared_heads, query_per_head, HEAD_WIDTH)
    all_pos = jnp.arange(all_tokens, dtype=jnp.int32)
    all_req, all_pre, _ = token_tables(request_prefix, suffix_lengths, all_pos, prefix_length)
    group_pre = jnp.repeat(
        lax.dynamic_slice_in_dim(slot_prefix, my_seq * blocks_here, blocks_here), block_rows
    )
    key_positions = my_seq * rows_here + jnp.arange(rows_here, dtype=jnp.int32)
    group_req, _, _ = token_tables(request_prefix, suffix_lengths, key_positions, prefix_length)
    all_keys = jnp.concatenate([cache_mine[..., :HEAD_WIDTH], pairs_mine[..., :HEAD_WIDTH]], axis=0)
    all_values = jnp.concatenate(
        [cache_mine[..., HEAD_WIDTH:], pairs_mine[..., HEAD_WIDTH:]], axis=0
    )
    key_pre = jnp.concatenate([group_pre, jnp.full((rows_here,), -1, jnp.int32)])
    key_req = jnp.concatenate([jnp.full((cache_extent,), -1, jnp.int32), group_req])
    key_pos = jnp.concatenate([jnp.zeros((cache_extent,), jnp.int32), key_positions])
    bundle = (all_keys, all_values, key_pre, key_req, key_pos)
    highest_score, total_weight, layer_output = tile_partials(
        query_all, all_req, all_pre, all_pos, bundle, min(512, all_tokens)
    )
    highest_score = highest_score.reshape(seq_count, rows_here, shared_heads, query_per_head)
    total_weight = total_weight.reshape(seq_count, rows_here, shared_heads, query_per_head)
    layer_output = layer_output.reshape(
        seq_count, rows_here, shared_heads, query_per_head, HEAD_WIDTH
    )
    widened = lax.optimization_barrier(layer_output).astype(jnp.float32)
    result_back, peak_back, total_back = (
        lax.all_to_all(widened, "seq", split_axis=0, concat_axis=0, tiled=True),
        lax.all_to_all(highest_score, "seq", split_axis=0, concat_axis=0, tiled=True),
        lax.all_to_all(total_weight, "seq", split_axis=0, concat_axis=0, tiled=True),
    )
    best_score = jnp.max(peak_back, axis=0)
    scaling = total_back * jnp.exp(peak_back - best_score[None])
    attended = (
        jnp.sum(scaling[..., None] * result_back, axis=0) / jnp.sum(scaling, axis=0)[..., None]
    )
    attended = attended.astype(jnp.bfloat16).reshape(rows_here, local_heads * HEAD_WIDTH)
    partial_out = jnp.dot(attended, w_out, preferred_element_type=jnp.float32)
    column_count = hidden_in.shape[1] // model_count
    summed = lax.psum(partial_out.astype(jnp.bfloat16), "mp").astype(jnp.float32)
    residual = (hidden_f32 + summed).astype(jnp.bfloat16)
    residual_cols = lax.dynamic_slice_in_dim(residual, my_model * column_count, column_count, 1)
    post_normed = row_norm(residual.astype(jnp.float32), post_gain).astype(jnp.bfloat16)
    gate_terms = jnp.dot(post_normed, w_gate, preferred_element_type=jnp.float32)
    up_terms = jnp.dot(post_normed, w_up, preferred_element_type=jnp.float32)
    middle = (jax.nn.silu(gate_terms) * up_terms).astype(jnp.bfloat16)
    down_terms = jnp.dot(middle, w_down, preferred_element_type=jnp.float32)
    hidden_part = lax.psum_scatter(
        down_terms.astype(jnp.bfloat16), "mp", scatter_dimension=1, tiled=True
    ).astype(jnp.float32)
    hidden_out = (residual_cols.astype(jnp.float32) + hidden_part).astype(jnp.bfloat16)
    return (hidden_out, suffix_key_values)


def solution(mesh):
    in_specs = (
        P("seq", None),
        P(),
        P(None, "mp"),
        P(None, "mp"),
        P(),
        P(),
        P("mp", None),
        P(),
        P(None, "mp"),
        P(None, "mp"),
        P("mp", None),
        P("seq", None, None, None),
        P(),
        P(),
        P(),
    )
    out_specs = (P("seq", "mp"), P("seq", "mp"))
    return jax.shard_map(local, mesh=mesh, in_specs=in_specs, out_specs=out_specs, check_vma=False)
```

profile of v0, /device:TPU:8, one launch (start us, length us, event | category | flops | bytes accessed | tf_op | source)
XLA Modules:
  0.0 402.8 jit_solution(13331135312913714287)
XLA Ops:
  7.3 1.4 fusion.20
  8.7 1.8 convolution_convert_fusion.2
  12.8 33.7 %all_gather.3 = bf16[2048,128]{0,1:T(8,128)(2,1)S(1)} all-gather(bf16[128,128]{0,1:T(8,128)(2,1)S(1)} %pad_maximum_fusion.3), channel_id=1, replica_groups=mesh['seq'=16,'mp'=16] {'seq'}, dimensions={0}, use_global_device_ids=true | all-gather | bytes 557056 | tf_op jit(solution)/shard_map/all_gather | solution.py:188
  47.5 33.2 %while.14 = (s32[]{:T(128)}, f32[4,512,1,1]{1,3,2,0:T(1,128)S(1)}, f32[4,512,1,1]{1,3,2,0:T(1,128)}, bf16[4,512,1,1,128]{4,1,3,2,0:T(8,128)(2,1)}, s32[640]{0:T(...) while((s32[]{:T(128)}, f32[4,512,1,1]{1,3,2,0:T(1,128)S(1)}, ...), condition=%wide.region_15.16_spmd, body=%wide.region_9.15_spmd.sunk | while | flops 172817920 | bytes 6144739 | solution.py:113
  49.2 4.6 %conditional.2 = (f32[1,512,1,1]{1,3,2,0:T(1,128)}, f32[1,512,1,1]{1,3,2,0:T(1,128)}, bf16[1,512,1,1,128]{4,1,3,2,0:T(8,128)(2,1)S(1)}) conditional(s32[]{:T(128)} %convert_element_type.195, () %tuple.64, (pred[512,640]{1,0:T(32,128)(4,1)S(1)}, bf16[4,512,1,1,128]{4,1,3,2,0:T(8,128)(2,1)S(1)}, s32[]{:T(128)}, bf16[640,1,128]{2,0,1:T(8,128)(2,1)S(1)}, ...), branch_computations={%region_11.11_spmd, %region_12.14_spmd} | conditional | flops 170851840 | bytes 5519388 | solution.py:111
  50.3 1.7 fusion.5
  52.7 1.1 fusion.3
  53.8 1.3 constant_dynamic-update-slice_fusion.5
  57.5 4.6 %conditional.2 = (f32[1,512,1,1]{1,3,2,0:T(1,128)}, f32[1,512,1,1]{1,3,2,0:T(1,128)}, bf16[1,512,1,1,128]{4,1,3,2,0:T(8,128)(2,1)S(1)}) conditional(s32[]{:T(128)} %convert_element_type.195, () %tuple.64, (pred[512,640]{1,0:T(32,128)(4,1)S(1)}, bf16[4,512,1,1,128]{4,1,3,2,0:T(8,128)(2,1)S(1)}, s32[]{:T(128)}, bf16[640,1,128]{2,0,1:T(8,128)(2,1)S(1)}, ...), branch_computations={%region_11.11_spmd, %region_12.14_spmd} | conditional | flops 170851840 | bytes 5519388 | solution.py:111
  58.6 1.7 fusion.5
  61.0 1.1 fusion.3
  62.1 1.3 constant_dynamic-update-slice_fusion.5
  65.8 4.6 %conditional.2 = (f32[1,512,1,1]{1,3,2,0:T(1,128)}, f32[1,512,1,1]{1,3,2,0:T(1,128)}, bf16[1,512,1,1,128]{4,1,3,2,0:T(8,128)(2,1)S(1)}) conditional(s32[]{:T(128)} %convert_element_type.195, () %tuple.64, (pred[512,640]{1,0:T(32,128)(4,1)S(1)}, bf16[4,512,1,1,128]{4,1,3,2,0:T(8,128)(2,1)S(1)}, s32[]{:T(128)}, bf16[640,1,128]{2,0,1:T(8,128)(2,1)S(1)}, ...), branch_computations={%region_11.11_spmd, %region_12.14_spmd} | conditional | flops 170851840 | bytes 5519388 | solution.py:111
  65.8 1.1 fusion.66
  66.9 1.7 fusion.5
  69.3 1.1 fusion.3
  70.4 1.3 constant_dynamic-update-slice_fusion.5
  74.1 4.6 %conditional.2 = (f32[1,512,1,1]{1,3,2,0:T(1,128)}, f32[1,512,1,1]{1,3,2,0:T(1,128)}, bf16[1,512,1,1,128]{4,1,3,2,0:T(8,128)(2,1)S(1)}) conditional(s32[]{:T(128)} %convert_element_type.195, () %tuple.64, (pred[512,640]{1,0:T(32,128)(4,1)S(1)}, bf16[4,512,1,1,128]{4,1,3,2,0:T(8,128)(2,1)S(1)}, s32[]{:T(128)}, bf16[640,1,128]{2,0,1:T(8,128)(2,1)S(1)}, ...), branch_computations={%region_11.11_spmd, %region_12.14_spmd} | conditional | flops 170851840 | bytes 5519388 | solution.py:111
  75.1 1.7 fusion.5
  77.6 1.1 fusion.3
  78.7 1.3 constant_dynamic-update-slice_fusion.5
  80.6 13.7 %all_to_all.15 = f32[16,128,1,1]{1,3,2,0:T(1,128)S(1)} all-to-all(f32[16,128,1,1]{1,3,2,0:T(1,128)S(1)} %bitcast.115), channel_id=1, replica_groups=mesh['seq'=16,'mp'=16] {'seq'}, dimensions={0} | all-to-all | bytes 16384 | tf_op jit(solution)/shard_map/all_to_all | solution.py:218
  94.3 4.7 %all-to-all-start = ((f32[16,128,1,1]{1,3,2,0:T(1,128)}), f32[16,128,1,1]{1,3,2,0:T(1,128)S(1)}, u32[]{:S(2)}, u32[]{:S(2)}) async-start(f32[16,128,1,1]{1,3,2,0:T(1,128)} %bitcast.29), calls=%async_computation | async-start | bytes 16384 | tf_op jit(solution)/shard_map/all_to_all | solution.py:219
  99.0 2.1 convert_element_type.121
  101.2 6.5 %all-to-all-done = f32[16,128,1,1]{1,3,2,0:T(1,128)S(1)} async-done(((f32[16,128,1,1]{1,3,2,0:T(1,128)}), f32[16,128,1,1]{1,3,2,0:T(1,128)S(1)}, u32[]{:S(2)}, u32[]{:S(2)}) %all-to-all-start) | async-done | bytes 8224 | tf_op jit(solution)/shard_map/all_to_all | solution.py:219
  107.6 4.9 %all-to-all-start.2 = ((f32[16,128,1,1,128]{4,1,3,2,0:T(8,128)}), f32[16,128,1,1,128]{4,1,3,2,0:T(8,128)S(1)}, u32[]{:S(2)}, u32[]{:S(2)}) async-start(f32[16,128,1,1,128]{4,1,3,2,0:T(8,128)} %convert_element_type.121), calls=%async_computation.2 | async-start | bytes 2097152 | tf_op jit(solution)/shard_map/all_to_all | solution.py:217
  112.6 23.0 %all-to-all-done.2 = f32[16,128,1,1,128]{4,1,3,2,0:T(8,128)S(1)} async-done(((f32[16,128,1,1,128]{4,1,3,2,0:T(8,128)}), f32[16,128,1,1,128]{4,1,3,2,0:T(8,128)S(1)}, u32[]{:S(2)}, u32[]{:S(2)}) %all-to-all-start.2) | async-done | bytes 1048608 | tf_op jit(solution)/shard_map/all_to_all | solution.py:217
  136.7 1.2 convolution_convert_fusion.1
  137.9 167.1 %all-reduce.5.cloned.1.call-done = bf16[128,2048]{1,0:T(8,128)(2,1)} async-done(((bf16[128,2048]{1,0:T(8,128)(2,1)}), bf16[128,2048]{1,0:T(8,128)(2,1)}) %all-reduce.5.cloned.1.call-update) | async-done | bytes 524304 | tf_op jit(solution)/shard_map/psum | solution.py:229
  305.0 1.4 fusion.17
  307.0 2.8 convolution_convert_fusion
  311.6 82.8 %reduce-scatter.4.cloned.1.call-done = bf16[128,128]{1,0:T(8,128)(2,1)} async-done(((bf16[2048,128]{1,0:T(8,128)(2,1)}), bf16[128,128]{1,0:T(8,128)(2,1)}) %reduce-scatter.4.cloned.1.call-update) | async-done | bytes 32784
  (110 shorter events, 20.9 us)
Async XLA Ops:
  7.2 39.6 %copy-start = (bf16[2,256,8,256]{3,2,1,0:T(8,128)(2,1)S(1)}, bf16[2,256,8,256]{3,2,1,0:T(8,128)(2,1)}, u32[]{:S(2)}) copy-start(bf16[2,256,8,256]{3,2,1,0:T(8,128)(2,1)} %param.30) | copy-start | bytes 6291460
  7.2 3.5 copy-start.12
  7.3 3.7 copy-start.6
  7.3 4.1 %copy-start.7 = (s32[32]{0:T(128)S(1)}, s32[32]{0:T(128)}, u32[]{:S(2)}) copy-start(s32[32]{0:T(128)} %param.32) | copy-start | bytes 388
  7.3 4.4 %copy-start.1 = (bf16[128,2048]{1,0:T(8,128)(2,1)S(1)}, bf16[128,2048]{1,0:T(8,128)(2,1)}, u32[]{:S(2)}) copy-start(bf16[128,2048]{1,0:T(8,128)(2,1)} %param.19) | copy-start | bytes 1572868
  7.3 4.4 %copy-start.9 = (bf16[2048,128]{1,0:T(8,128)(2,1)S(1)}, bf16[2048,128]{1,0:T(8,128)(2,1)}, u32[]{:S(2)}) copy-start(bf16[2048,128]{1,0:T(8,128)(2,1)} %param.21) | copy-start | bytes 1572868
  7.3 4.4 %copy-start.10 = (f32[2048]{0:T(1024)S(1)}, f32[2048]{0:T(1024)}, u32[]{:S(2)}) copy-start(f32[2048]{0:T(1024)} %param.20) | copy-start | bytes 24580
  10.5 1.6 copy-start.4
  10.5 1.7 copy-start.5
  94.3 13.3 %all-to-all-start = ((f32[16,128,1,1]{1,3,2,0:T(1,128)}), f32[16,128,1,1]{1,3,2,0:T(1,128)S(1)}, u32[]{:S(2)}, u32[]{:S(2)}) async-start(f32[16,128,1,1]{1,3,2,0:T(1,128)} %bitcast.29), calls=%async_computation | async-start | bytes 16384 | tf_op jit(solution)/shard_map/all_to_all | solution.py:219
  107.6 28.0 %all-to-all-start.2 = ((f32[16,128,1,1,128]{4,1,3,2,0:T(8,128)}), f32[16,128,1,1,128]{4,1,3,2,0:T(8,128)S(1)}, u32[]{:S(2)}, u32[]{:S(2)}) async-start(f32[16,128,1,1,128]{4,1,3,2,0:T(8,128)} %convert_element_type.121), calls=%async_computation.2 | async-start | bytes 2097152 | tf_op jit(solution)/shard_map/all_to_all | solution.py:217
  112.5 192.5 %all-reduce.5.cloned.1.call-start = ((), (), s32[]{:S(2)}) async-start(), calls=%async_computation.4 | async-start | bytes 1048576 | tf_op jit(solution)/shard_map/psum | solution.py:229
  135.6 1.0 copy-start.3
  136.0 169.0 %copy-start.2 = (bf16[128,2048]{1,0:T(8,128)(2,1)S(1)}, bf16[128,2048]{1,0:T(8,128)(2,1)}, u32[]{:S(2)}) copy-start(bf16[128,2048]{1,0:T(8,128)(2,1)} %param.19) | copy-start | bytes 1572868
  137.8 168.6 %copy-start.11 = (f32[2048]{0:T(1024)S(1)}, f32[2048]{0:T(1024)}, u32[]{:S(2)}) copy-start(f32[2048]{0:T(1024)} %param.26) | copy-start | bytes 24580
  137.9 256.6 %reduce-scatter.4.cloned.1.call-start = ((), (), s32[]{:S(2)}) async-start(), calls=%async_computation.5 | async-start | bytes 557056
  305.0 1.6 copy-start.8
Sparse Core Ops, SparseCore 0:
  138.0 166.9 all-reduce.4
  311.0 83.4 reduce-scatter.3
where the time goes:
time: 404 us; the launch traced here: 403 us
  waiting for transfers between devices  279 us (69%)
  blocking collectives  47.4 us (12%)
  other arithmetic  20.9 us (5%)
  matrix products  15.3 us (4%)
  between operations  14.5 us (4%)
  local copies, waits for them, and re-layouts  12.8 us (3%)
  starting transfers between devices  9.69 us (2%)
    psum x1, waiting for transfers between devices, local(): lax.psum(partial_out.astype(jnp.bfloat16), 'mp').astype(jnp.float32)  167 us
    unnamed x3, waiting for transfers between devices  82.9 us
    all_gather x1, blocking collectives, local(): lax.all_gather(query_rows_all.reshape(rows_here, local_heads * HEAD_WIDTH...  33.7 us
    all_to_all x1, waiting for transfers between devices, local(): lax.all_to_all(widened, 'seq', split_axis=0, concat_axis=0, tiled=True)  23 us
    all_to_all x1, blocking collectives, local(): lax.all_to_all(highest_score, 'seq', split_axis=0, concat_axis=0, tiled=T...  13.7 us
  transfers between devices with their start and end apart: 4, of which 4 were waited for; matrix products, arithmetic and copies ran while one was open for 1% of the time, Pallas kernels for 0%

commit v1 on v0

--- a/solution.py
+++ b/solution.py
@@ -226,7 +226,9 @@
     attended = attended.astype(jnp.bfloat16).reshape(rows_here, local_heads * HEAD_WIDTH)
     partial_out = jnp.dot(attended, w_out, preferred_element_type=jnp.float32)
     column_count = hidden_in.shape[1] // model_count
-    summed = lax.psum(partial_out.astype(jnp.bfloat16), "mp").astype(jnp.float32)
+    summed = jnp.sum(lax.all_gather(partial_out.astype(jnp.bfloat16), "mp"), axis=0).astype(
+        jnp.float32
+    )
     residual = (hidden_f32 + summed).astype(jnp.bfloat16)
     residual_cols = lax.dynamic_slice_in_dim(residual, my_model * column_count, column_count, 1)
     post_normed = row_norm(residual.astype(jnp.float32), post_gain).astype(jnp.bfloat16)

time: 404 us -> 349 us (0.86)
  waiting for transfers between devices: 279 us -> 218 us
  other arithmetic: 20.9 us -> 25.8 us
    psum x1 -> x0, waiting for transfers between devices: 167 us -> none  [local(): lax.psum(partial_out.astype(jnp.bfloat16), 'mp').astype(jnp.float32)]
    all_gather x0 -> x1, waiting for transfers between devices: none -> 107 us  [local(): lax.all_gather(partial_out.astype(jnp.bfloat16), 'mp')]
    reduce_sum x0 -> x1, other arithmetic: none -> 5.3 us  [local(): jnp.sum(lax.all_gather(partial_out.astype(jnp.bfloat16), 'mp'), axis=0)]
where the time goes in v1:
time: 349 us; the launch traced here: 348 us
  waiting for transfers between devices  218 us (62%)
  blocking collectives  47.4 us (14%)
  other arithmetic  25.8 us (7%)
  matrix products  15.5 us (4%)
  between operations  14.5 us (4%)
  local copies, waits for them, and re-layouts  14 us (4%)
  starting transfers between devices  9.69 us (3%)
    all_gather x1, waiting for transfers between devices, local(): lax.all_gather(partial_out.astype(jnp.bfloat16), 'mp')  107 us
    unnamed x3, waiting for transfers between devices  81.3 us
    all_gather x1, blocking collectives, local(): lax.all_gather(query_rows_all.reshape(rows_here, local_heads * HEAD_WIDTH...  33.7 us
    all_to_all x1, waiting for transfers between devices, local(): lax.all_to_all(widened, 'seq', split_axis=0, concat_axis=0, tiled=True)  23 us
    all_to_all x1, blocking collectives, local(): lax.all_to_all(highest_score, 'seq', split_axis=0, concat_axis=0, tiled=T...  13.7 us
    dynamic_update_slice x8, local copies, waits for them, and re-layouts, tile_partials(): highest_score, total_weight, layer_output = lax.map(one_tile, shaped)  7.72 us
  transfers between devices with their start and end apart: 4, of which 4 were waited for; matrix products, arithmetic and copies ran while one was open for 1% of the time, Pallas kernels for 0%

profile of v1, /device:TPU:8, one launch (start us, length us, event | category | flops | bytes accessed | tf_op | source)
XLA Modules:
  0.0 347.8 jit_solution(13121832361025031860)
XLA Ops:
  7.3 1.4 fusion.20
  8.7 1.8 convolution_convert_fusion.2
  12.8 33.7 %all_gather.9 = bf16[2048,128]{0,1:T(8,128)(2,1)S(1)} all-gather(bf16[128,128]{0,1:T(8,128)(2,1)S(1)} %pad_maximum_fusion.3), channel_id=1, replica_groups=mesh['seq'=16,'mp'=16] {'seq'}, dimensions={0}, use_global_device_ids=true | all-gather | bytes 557056 | tf_op jit(solution)/shard_map/all_gather | solution.py:188
  47.5 33.2 %while.14 = (s32[]{:T(128)}, f32[4,512,1,1]{1,3,2,0:T(1,128)S(1)}, f32[4,512,1,1]{1,3,2,0:T(1,128)}, bf16[4,512,1,1,128]{4,1,3,2,0:T(8,128)(2,1)}, s32[640]{0:T(...) while((s32[]{:T(128)}, f32[4,512,1,1]{1,3,2,0:T(1,128)S(1)}, ...), condition=%wide.region_15.16_spmd, body=%wide.region_9.15_spmd.sunk | while | flops 172817920 | bytes 6144739 | solution.py:113
  49.2 4.6 %conditional.2 = (f32[1,512,1,1]{1,3,2,0:T(1,128)}, f32[1,512,1,1]{1,3,2,0:T(1,128)}, bf16[1,512,1,1,128]{4,1,3,2,0:T(8,128)(2,1)S(1)}) conditional(s32[]{:T(128)} %convert_element_type.197, () %tuple.64, (pred[512,640]{1,0:T(32,128)(4,1)S(1)}, bf16[4,512,1,1,128]{4,1,3,2,0:T(8,128)(2,1)S(1)}, s32[]{:T(128)}, bf16[640,1,128]{2,0,1:T(8,128)(2,1)S(1)}, ...), branch_computations={%region_11.11_spmd, %region_12.14_spmd} | conditional | flops 170851840 | bytes 5519388 | solution.py:111
  50.3 1.7 fusion.5
  52.7 1.1 fusion.3
  53.8 1.3 constant_dynamic-update-slice_fusion.5
  57.5 4.6 %conditional.2 = (f32[1,512,1,1]{1,3,2,0:T(1,128)}, f32[1,512,1,1]{1,3,2,0:T(1,128)}, bf16[1,512,1,1,128]{4,1,3,2,0:T(8,128)(2,1)S(1)}) conditional(s32[]{:T(128)} %convert_element_type.197, () %tuple.64, (pred[512,640]{1,0:T(32,128)(4,1)S(1)}, bf16[4,512,1,1,128]{4,1,3,2,0:T(8,128)(2,1)S(1)}, s32[]{:T(128)}, bf16[640,1,128]{2,0,1:T(8,128)(2,1)S(1)}, ...), branch_computations={%region_11.11_spmd, %region_12.14_spmd} | conditional | flops 170851840 | bytes 5519388 | solution.py:111
  58.6 1.7 fusion.5
  61.0 1.1 fusion.3
  62.1 1.3 constant_dynamic-update-slice_fusion.5
  65.8 4.6 %conditional.2 = (f32[1,512,1,1]{1,3,2,0:T(1,128)}, f32[1,512,1,1]{1,3,2,0:T(1,128)}, bf16[1,512,1,1,128]{4,1,3,2,0:T(8,128)(2,1)S(1)}) conditional(s32[]{:T(128)} %convert_element_type.197, () %tuple.64, (pred[512,640]{1,0:T(32,128)(4,1)S(1)}, bf16[4,512,1,1,128]{4,1,3,2,0:T(8,128)(2,1)S(1)}, s32[]{:T(128)}, bf16[640,1,128]{2,0,1:T(8,128)(2,1)S(1)}, ...), branch_computations={%region_11.11_spmd, %region_12.14_spmd} | conditional | flops 170851840 | bytes 5519388 | solution.py:111
  66.9 1.7 fusion.5
  69.3 1.1 fusion.3
  70.4 1.3 constant_dynamic-update-slice_fusion.5
  74.1 4.6 %conditional.2 = (f32[1,512,1,1]{1,3,2,0:T(1,128)}, f32[1,512,1,1]{1,3,2,0:T(1,128)}, bf16[1,512,1,1,128]{4,1,3,2,0:T(8,128)(2,1)S(1)}) conditional(s32[]{:T(128)} %convert_element_type.197, () %tuple.64, (pred[512,640]{1,0:T(32,128)(4,1)S(1)}, bf16[4,512,1,1,128]{4,1,3,2,0:T(8,128)(2,1)S(1)}, s32[]{:T(128)}, bf16[640,1,128]{2,0,1:T(8,128)(2,1)S(1)}, ...), branch_computations={%region_11.11_spmd, %region_12.14_spmd} | conditional | flops 170851840 | bytes 5519388 | solution.py:111
  75.1 1.7 fusion.5
  77.6 1.1 fusion.3
  78.7 1.3 constant_dynamic-update-slice_fusion.5
  80.6 13.7 %all_to_all.15 = f32[16,128,1,1]{1,3,2,0:T(1,128)S(1)} all-to-all(f32[16,128,1,1]{1,3,2,0:T(1,128)S(1)} %bitcast.117), channel_id=1, replica_groups=mesh['seq'=16,'mp'=16] {'seq'}, dimensions={0} | all-to-all | bytes 16384 | tf_op jit(solution)/shard_map/all_to_all | solution.py:218
  94.3 4.7 %all-to-all-start = ((f32[16,128,1,1]{1,3,2,0:T(1,128)}), f32[16,128,1,1]{1,3,2,0:T(1,128)S(1)}, u32[]{:S(2)}, u32[]{:S(2)}) async-start(f32[16,128,1,1]{1,3,2,0:T(1,128)} %bitcast.29), calls=%async_computation | async-start | bytes 16384 | tf_op jit(solution)/shard_map/all_to_all | solution.py:219
  99.0 2.1 convert_element_type.123
  101.2 6.5 %all-to-all-done = f32[16,128,1,1]{1,3,2,0:T(1,128)S(1)} async-done(((f32[16,128,1,1]{1,3,2,0:T(1,128)}), f32[16,128,1,1]{1,3,2,0:T(1,128)S(1)}, u32[]{:S(2)}, u32[]{:S(2)}) %all-to-all-start) | async-done | bytes 8224 | tf_op jit(solution)/shard_map/all_to_all | solution.py:219
  107.6 4.9 %all-to-all-start.2 = ((f32[16,128,1,1,128]{4,1,3,2,0:T(8,128)}), f32[16,128,1,1,128]{4,1,3,2,0:T(8,128)S(1)}, u32[]{:S(2)}, u32[]{:S(2)}) async-start(f32[16,128,1,1,128]{4,1,3,2,0:T(8,128)} %convert_element_type.123), calls=%async_computation.2 | async-start | bytes 2097152 | tf_op jit(solution)/shard_map/all_to_all | solution.py:217
  112.6 23.0 %all-to-all-done.2 = f32[16,128,1,1,128]{4,1,3,2,0:T(8,128)S(1)} async-done(((f32[16,128,1,1,128]{4,1,3,2,0:T(8,128)}), f32[16,128,1,1,128]{4,1,3,2,0:T(8,128)S(1)}, u32[]{:S(2)}, u32[]{:S(2)}) %all-to-all-start.2) | async-done | bytes 1048608 | tf_op jit(solution)/shard_map/all_to_all | solution.py:217
  136.7 1.2 convolution_convert_fusion.1
  137.9 107.3 %all-gather.3.cloned.1.call-done = bf16[2048,2048]{1,0:T(8,128)(2,1)} async-done(((bf16[128,2048]{1,0:T(8,128)(2,1)}), bf16[2048,2048]{1,0:T(8,128)(2,1)}) %all-gather.3.cloned.1.call-update) | async-done | bytes 8388624 | tf_op jit(solution)/shard_map/all_gather | solution.py:229
  245.2 5.3 %reduce_sum.130 = bf16[128,2048]{1,0:T(8,128)(2,1)S(1)} reduce(bf16[16,128,2048]{2,1,0:T(8,128)(2,1)} %bitcast.101, bf16[]{:T(256)} %constant.118.clone.1), dimensions={0}, to_apply=%region_19.20 | reduce | flops 3932160 | bytes 8912898 | tf_op jit(solution)/shard_map/reduce_sum | solution.py:229
  252.6 2.9 convolution_convert_fusion
  257.4 81.3 %reduce-scatter.4.cloned.1.call-done = bf16[128,128]{1,0:T(8,128)(2,1)} async-done(((bf16[2048,128]{1,0:T(8,128)(2,1)}), bf16[128,128]{1,0:T(8,128)(2,1)}) %reduce-scatter.4.cloned.1.call-update) | async-done | bytes 32784
  339.5 1.4 add_convert_fusion
  (113 shorter events, 22.8 us)
Async XLA Ops:
  7.2 39.6 %copy-start = (bf16[2,256,8,256]{3,2,1,0:T(8,128)(2,1)S(1)}, bf16[2,256,8,256]{3,2,1,0:T(8,128)(2,1)}, u32[]{:S(2)}) copy-start(bf16[2,256,8,256]{3,2,1,0:T(8,128)(2,1)} %param.30) | copy-start | bytes 6291460
  7.2 3.5 copy-start.13
  7.3 3.7 %copy-start.7 = (s32[32]{0:T(128)S(1)}, s32[32]{0:T(128)}, u32[]{:S(2)}) copy-start(s32[32]{0:T(128)} %param.33) | copy-start | bytes 388
  7.3 4.1 %copy-start.8 = (s32[32]{0:T(128)S(1)}, s32[32]{0:T(128)}, u32[]{:S(2)}) copy-start(s32[32]{0:T(128)} %param.32) | copy-start | bytes 388
  7.3 4.4 %copy-start.1 = (bf16[128,2048]{1,0:T(8,128)(2,1)S(1)}, bf16[128,2048]{1,0:T(8,128)(2,1)}, u32[]{:S(2)}) copy-start(bf16[128,2048]{1,0:T(8,128)(2,1)} %param.19) | copy-start | bytes 1572868
  7.3 4.4 %copy-start.10 = (bf16[2048,128]{1,0:T(8,128)(2,1)S(1)}, bf16[2048,128]{1,0:T(8,128)(2,1)}, u32[]{:S(2)}) copy-start(bf16[2048,128]{1,0:T(8,128)(2,1)} %param.21) | copy-start | bytes 1572868
  7.3 4.4 %copy-start.11 = (f32[2048]{0:T(1024)S(1)}, f32[2048]{0:T(1024)}, u32[]{:S(2)}) copy-start(f32[2048]{0:T(1024)} %param.20) | copy-start | bytes 24580
  10.5 1.6 copy-start.5
  10.5 1.7 copy-start.6
  94.3 13.3 %all-to-all-start = ((f32[16,128,1,1]{1,3,2,0:T(1,128)}), f32[16,128,1,1]{1,3,2,0:T(1,128)S(1)}, u32[]{:S(2)}, u32[]{:S(2)}) async-start(f32[16,128,1,1]{1,3,2,0:T(1,128)} %bitcast.29), calls=%async_computation | async-start | bytes 16384 | tf_op jit(solution)/shard_map/all_to_all | solution.py:219
  107.6 28.0 %all-to-all-start.2 = ((f32[16,128,1,1,128]{4,1,3,2,0:T(8,128)}), f32[16,128,1,1,128]{4,1,3,2,0:T(8,128)S(1)}, u32[]{:S(2)}, u32[]{:S(2)}) async-start(f32[16,128,1,1,128]{4,1,3,2,0:T(8,128)} %convert_element_type.123), calls=%async_computation.2 | async-start | bytes 2097152 | tf_op jit(solution)/shard_map/all_to_all | solution.py:217
  112.5 132.7 %all-gather.3.cloned.1.call-start = ((), (), s32[]{:S(2)}) async-start(), calls=%async_computation.4 | async-start | bytes 8912896 | tf_op jit(solution)/shard_map/all_gather | solution.py:229
  135.6 1.0 copy-start.4
  137.9 200.8 %reduce-scatter.4.cloned.1.call-start = ((), (), s32[]{:S(2)}) async-start(), calls=%async_computation.5 | async-start | bytes 557056
  245.2 5.3 %copy-start.2 = (bf16[128,2048]{1,0:T(8,128)(2,1)S(1)}, bf16[128,2048]{1,0:T(8,128)(2,1)}, u32[]{:S(2)}) copy-start(bf16[128,2048]{1,0:T(8,128)(2,1)} %param.19) | copy-start | bytes 1572868
  245.2 6.4 %copy-start.12 = (f32[2048]{0:T(1024)S(1)}, f32[2048]{0:T(1024)}, u32[]{:S(2)}) copy-start(f32[2048]{0:T(1024)} %param.26) | copy-start | bytes 24580
  250.5 1.6 copy-start.9
  250.8 0.8 copy-start.3
Sparse Core Ops, SparseCore 0:
  138.0 107.1 all-gather.2
  256.7 81.8 reduce-scatter.3
